TPU v7x, 32 devices: a whole 2x2x4 slice. The times are simulated.
32 devices in a mesh: dp: 16 (over z, y, core), mp: 2 (over x).
Axes of the slice: x: 2, y: 2, z: 4, core: 2. Of those that a mesh axis runs over, the one named last changes fastest.
Arguments:
- activations: bfloat16 [2, 16384, 512], P(None, 'dp'), may hold values from -6 to 6
- cotangent: bfloat16 [2, 16384, 512], P(None, 'dp'), may hold values from -6 to 6
- w_qkv: bfloat16 [3, 512, 512], P(None, 'dp', 'mp'), may hold values from -0.25 to 0.25
- w_o: bfloat16 [512, 512], P('mp', 'dp'), may hold values from -0.75 to 0.75
- w_up: bfloat16 [512, 2048], P('dp', 'mp'), may hold values from -0.25 to 0.25
- w_down: bfloat16 [2048, 512], P('mp', 'dp'), may hold values from -0.125 to 0.125
- b_qv: bfloat16 [2, 8, 64], P(None, 'mp', 'dp'), may hold values from -3 to 3
- b_up: bfloat16 [32, 64], P('mp', 'dp'), may hold values from -3 to 3
- out_bias: bfloat16 [2, 512], P(None, 'dp'), may hold values from -3 to 3
- norm_gain: bfloat16 [2, 512], P(None, 'dp'), may hold values from 0.25 to 1.75
- norm_bias: bfloat16 [2, 512], P(None, 'dp'), may hold values from -2 to 2
- chain_ids: int32 [2, 16384], P(None, 'dp'), may hold values from -1 to 1023, as said below
- key_keep: int32 [2, 16384], P(None, 'dp'), may hold values 0 or 1
Outputs:
- output: float32 [2, 16384, 512], P(None, 'dp')
- grad_x: float32 [2, 16384, 512], P(None, 'dp')
- grad_w_qkv: float32 [3, 512, 512], P(None, 'dp', 'mp')
- grad_w_o: float32 [512, 512], P('mp', 'dp')
- grad_w_up: float32 [512, 2048], P('dp', 'mp')
- grad_w_down: float32 [2048, 512], P('mp', 'dp')
- grad_b_qv: float32 [2, 8, 64], P(None, 'mp', 'dp')
- grad_b_up: float32 [32, 64], P('mp', 'dp')
- grad_out_bias: float32 [2, 512], P(None, 'dp')
- grad_norm_gain: float32 [2, 512], P(None, 'dp')
- grad_norm_bias: float32 [2, 512], P(None, 'dp')
Inputs may be any that keep to these rules, and one draw needn't show every extreme that they name: `chain_ids`: in each aligned block of 1024 slots along the last dimension, a live slot carries the index within the block of the first slot of its chain, chains are contiguous runs of live slots, the first slot of every block is live, and padding slots (-1) come after all live slots of their block; how many slots are live differs from block to block.
All inputs are finite; a program needn't handle non-finite values. No bound on the sum of `key_keep` on one device may be relied on, other than what follows from the above.
Results may differ from a plain program's by a relative error of at most 0.018.
Values may be sent and summed in bfloat16 or wider, within the bound.
A program may use at most 192 MiB of HBM per device.

v0:
```python
import math
import jax
import jax.numpy as jnp
from jax import lax
from jax.sharding import PartitionSpec as P

epsilon = 1e-05
masked_value = -1e30


def product(left, right):
    return jnp.dot(left, right, preferred_element_type=jnp.float32)


def normalize(values, scale_row, shift_row):
    row_mean = jnp.mean(values, axis=-1, keepdims=True)
    centred = values - row_mean
    inverse = lax.rsqrt(jnp.mean(centred * centred, axis=-1, keepdims=True) + epsilon)
    scaled = centred * inverse
    return (scaled * scale_row + shift_row, scaled, inverse)


def normalize_back(grad_rows, scaled, inverse, scale_row):
    inner = grad_rows * scale_row
    return inverse * (
        inner
        - jnp.mean(inner, axis=-1, keepdims=True)
        - scaled * jnp.mean(inner * scaled, axis=-1, keepdims=True)
    )


def gelu_slope(values):
    normal_cdf = 0.5 * (1.0 + lax.erf(values * 0.7071067811865476))
    density = jnp.exp(-0.5 * values * values) * 0.3989422804014327
    return normal_cdf + values * density


def permitted(chain_rows, keep_rows):
    slot_count = chain_rows.shape[0]
    same_chain = chain_rows[:, None] == chain_rows[None, :]
    diagonal = lax.broadcasted_iota(jnp.int32, (slot_count, slot_count), 0) == lax.broadcasted_iota(
        jnp.int32, (slot_count, slot_count), 1
    )
    return same_chain & ((keep_rows[None, :] == 1) | diagonal)


def head_scores(query, key_rows, allowed, head_count, head_width):
    query_heads = query.reshape(-1, head_count, head_width)
    key_heads = key_rows.reshape(-1, head_count, head_width)
    scores = jnp.einsum(
        "qhd,khd->hqk", query_heads, key_heads, preferred_element_type=jnp.float32
    ) * (1.0 / math.sqrt(head_width))
    return jnp.where(allowed[None], scores, masked_value)


def forward(rows_in, chain_rows, keep_rows, weights):
    qkv_full, out_full, up_full, down_full, bias_qv, bias_up, bias_out, gain_full, shift_full = (
        weights
    )
    head_count = bias_qv.shape[1]
    head_width = bias_qv.shape[2]
    row_count = rows_in.shape[0]
    bias_qv = bias_qv.astype(jnp.float32)
    bias_out = bias_out.astype(jnp.float32)
    gain_full = gain_full.astype(jnp.float32)
    shift_full = shift_full.astype(jnp.float32)
    allowed = permitted(chain_rows, keep_rows)
    normed_one, scaled_one, inverse_one = normalize(rows_in, gain_full[0], shift_full[0])
    hidden_one = normed_one.astype(jnp.bfloat16)
    query = (product(hidden_one, qkv_full[0]) + bias_qv[0].reshape(-1)).astype(jnp.bfloat16)
    key_rows = product(hidden_one, qkv_full[1]).astype(jnp.bfloat16)
    value_rows = (product(hidden_one, qkv_full[2]) + bias_qv[1].reshape(-1)).astype(jnp.bfloat16)
    scores = head_scores(query, key_rows, allowed, head_count, head_width)
    row_top = jnp.max(scores, axis=-1, keepdims=True)
    log_total = jnp.log(jnp.sum(jnp.exp(scores - row_top), axis=-1, keepdims=True)) + row_top
    probs_low = jnp.exp(scores - log_total).astype(jnp.bfloat16)
    mixed = jnp.einsum(
        "hqk,khd->qhd",
        probs_low,
        value_rows.reshape(row_count, head_count, head_width),
        preferred_element_type=jnp.float32,
    )
    mixed = mixed.reshape(row_count, -1).astype(jnp.bfloat16)
    partial_attn = product(mixed, out_full)
    resid = rows_in + lax.psum(partial_attn, "mp") + bias_out[0]
    normed_two, scaled_two, inverse_two = normalize(resid, gain_full[1], shift_full[1])
    hidden_two = normed_two.astype(jnp.bfloat16)
    pre = product(hidden_two, up_full) + bias_up.astype(jnp.float32).reshape(-1)
    act = jax.nn.gelu(pre, approximate=False).astype(jnp.bfloat16)
    partial_ffn = product(act, down_full)
    result = (
        resid + lax.psum(partial_ffn.astype(jnp.bfloat16), "mp").astype(jnp.float32) + bias_out[1]
    )
    kept = (
        allowed,
        scaled_one,
        inverse_one,
        hidden_one,
        query,
        key_rows,
        value_rows,
        log_total,
        mixed,
        scaled_two,
        inverse_two,
        hidden_two,
        pre,
        act,
    )
    return (result, kept)


def backward(grad_out, result, kept, weights):
    qkv_full, out_full, up_full, down_full, bias_qv, bias_up, bias_out, gain_full, shift_full = (
        weights
    )
    (
        allowed,
        scaled_one,
        inverse_one,
        hidden_one,
        query,
        key_rows,
        value_rows,
        log_total,
        mixed,
        scaled_two,
        inverse_two,
        hidden_two,
        pre,
        act,
    ) = kept
    head_count = bias_qv.shape[1]
    head_width = bias_qv.shape[2]
    row_count = grad_out.shape[0]
    gain_full = gain_full.astype(jnp.float32)
    grad_low = grad_out.astype(jnp.bfloat16)
    grad_down = product(act.T, grad_low)
    grad_pre = (product(grad_low, down_full.T) * gelu_slope(pre)).astype(jnp.bfloat16)
    grad_bup = jnp.sum(grad_pre, axis=0, dtype=jnp.float32).reshape(bias_up.shape)
    grad_up = product(hidden_two.T, grad_pre)
    partial_two = product(grad_pre, up_full.T)
    grad_two = lax.psum(partial_two.astype(jnp.bfloat16), "mp").astype(jnp.float32)
    gain_two = jnp.sum(grad_two * scaled_two, axis=0)
    shift_two = jnp.sum(grad_two, axis=0)
    grad_resid = grad_out + normalize_back(grad_two, scaled_two, inverse_two, gain_full[1])
    resid_low = grad_resid.astype(jnp.bfloat16)
    grad_out_proj = product(mixed.T, resid_low)
    grad_mixed = (
        product(resid_low, out_full.T)
        .astype(jnp.bfloat16)
        .reshape(row_count, head_count, head_width)
    )
    scores = head_scores(query, key_rows, allowed, head_count, head_width)
    probs = jnp.exp(scores - log_total)
    probs_low = probs.astype(jnp.bfloat16)
    value_heads = value_rows.reshape(row_count, head_count, head_width)
    grad_value = jnp.einsum(
        "hqk,qhd->khd", probs_low, grad_mixed, preferred_element_type=jnp.float32
    ).astype(jnp.bfloat16)
    grad_probs = jnp.einsum(
        "qhd,khd->hqk", grad_mixed, value_heads, preferred_element_type=jnp.float32
    )
    grad_scores = (
        probs * (grad_probs - jnp.sum(grad_probs * probs, axis=-1, keepdims=True))
    ).astype(jnp.bfloat16)
    score_scale = 1.0 / math.sqrt(head_width)
    key_heads = key_rows.reshape(row_count, head_count, head_width)
    query_heads = query.reshape(row_count, head_count, head_width)
    grad_query = (
        jnp.einsum("hqk,khd->qhd", grad_scores, key_heads, preferred_element_type=jnp.float32)
        * score_scale
    ).astype(jnp.bfloat16)
    grad_key = (
        jnp.einsum("hqk,qhd->khd", grad_scores, query_heads, preferred_element_type=jnp.float32)
        * score_scale
    ).astype(jnp.bfloat16)
    stacked = jnp.stack(
        [
            grad_query.reshape(row_count, -1),
            grad_key.reshape(row_count, -1),
            grad_value.reshape(row_count, -1),
        ]
    )
    grad_qkv = jnp.einsum("rd,crk->cdk", hidden_one, stacked, preferred_element_type=jnp.float32)
    partial_one = jnp.einsum("crk,cdk->rd", stacked, qkv_full, preferred_element_type=jnp.float32)
    grad_one = lax.psum(partial_one.astype(jnp.bfloat16), "mp").astype(jnp.float32)
    grad_bqv = jnp.stack(
        [
            jnp.sum(stacked[0], axis=0, dtype=jnp.float32),
            jnp.sum(stacked[2], axis=0, dtype=jnp.float32),
        ]
    ).reshape(2, head_count, head_width)
    gain_one = jnp.sum(grad_one * scaled_one, axis=0)
    shift_one = jnp.sum(grad_one, axis=0)
    grad_in = grad_resid + normalize_back(grad_one, scaled_one, inverse_one, gain_full[0])
    small_sums = jnp.stack(
        [
            jnp.sum(grad_resid, axis=0),
            jnp.sum(grad_out, axis=0),
            gain_one,
            gain_two,
            shift_one,
            shift_two,
        ]
    )
    local_grads = (
        grad_qkv,
        grad_out_proj,
        grad_up,
        grad_down,
        grad_bqv,
        grad_bup,
        small_sums[0:2],
        small_sums[2:4],
        small_sums[4:6],
    )
    return (result, grad_in, local_grads)


def body(
    activations,
    cotangent,
    w_qkv,
    w_o,
    w_up,
    w_down,
    b_qv,
    b_up,
    out_bias,
    norm_gain,
    norm_bias,
    chain_ids,
    key_keep,
):
    batch_count = activations.shape[0]
    outputs = []
    input_grads = []
    running = None
    for batch_index in range(batch_count):
        weights = (
            lax.all_gather(w_qkv, "dp", axis=1, tiled=True),
            lax.all_gather(w_o, "dp", axis=1, tiled=True),
            lax.all_gather(w_up, "dp", axis=0, tiled=True),
            lax.all_gather(w_down, "dp", axis=1, tiled=True),
            lax.all_gather(b_qv, "dp", axis=2, tiled=True),
            lax.all_gather(b_up, "dp", axis=1, tiled=True),
            lax.all_gather(out_bias, "dp", axis=1, tiled=True),
            lax.all_gather(norm_gain, "dp", axis=1, tiled=True),
            lax.all_gather(norm_bias, "dp", axis=1, tiled=True),
        )
        result, kept = forward(
            activations[batch_index].astype(jnp.float32),
            chain_ids[batch_index],
            key_keep[batch_index],
            weights,
        )
        live_rows = (chain_ids[batch_index] >= 0).astype(jnp.float32)[:, None]
        output_rows, grad_in, local_grads = backward(
            cotangent[batch_index].astype(jnp.float32) * live_rows, result, kept, weights
        )
        outputs.append(output_rows)
        input_grads.append(grad_in)
        shares = (
            lax.psum_scatter(
                local_grads[0].astype(jnp.bfloat16), "dp", scatter_dimension=1, tiled=True
            ).astype(jnp.float32),
            lax.psum_scatter(
                local_grads[1].astype(jnp.bfloat16), "dp", scatter_dimension=1, tiled=True
            ).astype(jnp.float32),
            lax.psum_scatter(
                local_grads[2].astype(jnp.bfloat16), "dp", scatter_dimension=0, tiled=True
            ).astype(jnp.float32),
            lax.psum_scatter(
                local_grads[3].astype(jnp.bfloat16), "dp", scatter_dimension=1, tiled=True
            ).astype(jnp.float32),
            lax.psum_scatter(
                local_grads[4].astype(jnp.bfloat16), "dp", scatter_dimension=2, tiled=True
            ).astype(jnp.float32),
            lax.psum_scatter(
                local_grads[5].astype(jnp.bfloat16), "dp", scatter_dimension=1, tiled=True
            ).astype(jnp.float32),
            lax.psum_scatter(
                local_grads[6].astype(jnp.bfloat16), "dp", scatter_dimension=1, tiled=True
            ).astype(jnp.float32),
            lax.psum_scatter(
                local_grads[7].astype(jnp.bfloat16), "dp", scatter_dimension=1, tiled=True
            ).astype(jnp.float32),
            lax.psum_scatter(
                local_grads[8].astype(jnp.bfloat16), "dp", scatter_dimension=1, tiled=True
            ).astype(jnp.float32),
        )
        if running is None:
            running = tuple(shares)
        else:
            running = tuple(jax.tree.map(jnp.add, tuple(running), tuple(shares)))
    return (
        jnp.stack(outputs),
        jnp.stack(input_grads),
        running[0],
        running[1],
        running[2],
        running[3],
        running[4],
        running[5],
        running[6],
        running[7],
        running[8],
    )


def solution(mesh):
    placed = (
        P(None, "dp", None),
        P(None, "dp", None),
        P(None, "dp", "mp"),
        P("mp", "dp"),
        P("dp", "mp"),
        P("mp", "dp"),
        P(None, "mp", "dp"),
        P("mp", "dp"),
        P(None, "dp"),
        P(None, "dp"),
        P(None, "dp"),
        P(None, "dp"),
        P(None, "dp"),
    )
    return jax.shard_map(
        body,
        mesh=mesh,
        in_specs=placed,
        out_specs=(
            P(None, "dp", None),
            P(None, "dp", None),
            P(None, "dp", "mp"),
            P("mp", "dp"),
            P("dp", "mp"),
            P("mp", "dp"),
            P(None, "mp", "dp"),
            P("mp", "dp"),
            P(None, "dp"),
            P(None, "dp"),
            P(None, "dp"),
        ),
        check_vma=False,
    )
```

profile of v0, /device:TPU:0, one launch (start us, length us, event | category | flops | bytes accessed | tf_op | source)
XLA Modules:
  0.0 1243.1 jit_solution(9962415222344937010)
XLA Ops:
  9.0 23.3 %all-gather = bf16[16,32,2]{1,2,0:T(2,128)(2,1)S(1)} all-gather(bf16[1,32,2]{1,2,0:T(2,128)(2,1)} %bitcast.362), channel_id=1, replica_groups=mesh['dp'=16,'mp'=2] {'dp'}, dimensions={0}, use_global_device_ids=true | all-gather | bytes 2176 | tf_op jit(solution)/shard_map/all_gather | solution.py:249
  32.4 17.6 %all-gather.1 = bf16[16,32,2]{1,2,0:T(2,128)(2,1)S(1)} all-gather(bf16[1,32,2]{1,2,0:T(2,128)(2,1)} %bitcast.363), channel_id=1, replica_groups=mesh['dp'=16,'mp'=2] {'dp'}, dimensions={0}, use_global_device_ids=true | all-gather | bytes 2176 | tf_op jit(solution)/shard_map/all_gather | solution.py:250
  52.0 2.4 fusion.70
  54.5 18.8 %all_gather.39 = bf16[2,4,64]{1,0,2:T(2,128)(2,1)S(1)} all-gather(bf16[2,4,4]{1,0,2:T(2,128)(2,1)S(1)} %copy.117), channel_id=1, replica_groups=mesh['dp'=16,'mp'=2] {'dp'}, dimensions={2}, use_global_device_ids=true | all-gather | bytes 1088 | tf_op jit(solution)/shard_map/all_gather | solution.py:246
  73.7 19.6 %all_gather.38 = bf16[3,512,256]{2,1,0:T(8,128)(2,1)S(1)} all-gather(bf16[3,32,256]{2,1,0:T(8,128)(2,1)S(1)} %copy-done.61), channel_id=1, replica_groups=mesh['dp'=16,'mp'=2] {'dp'}, dimensions={1}, use_global_device_ids=true | all-gather | bytes 835584 | tf_op jit(solution)/shard_map/all_gather | solution.py:242
  99.8 19.8 %all_gather.40 = bf16[256,512]{0,1:T(8,128)(2,1)S(1)} all-gather(bf16[256,32]{0,1:T(8,128)(2,1)S(1)} %copy-done.64), channel_id=1, replica_groups=mesh['dp'=16,'mp'=2] {'dp'}, dimensions={1}, use_global_device_ids=true | all-gather | bytes 278528 | tf_op jit(solution)/shard_map/all_gather | solution.py:243
  119.6 2.4 fusion.36
  122.0 3.3 fusion.1
  125.4 3.7 exponential_reduce_fusion
  131.1 3.3 fusion
  134.4 3.7 exponential_reduce_fusion.1
  138.2 10.3 convolution_convert_fusion.14
  150.3 4.6 convolution_convert_fusion.16
  158.8 17.4 %all-gather.2 = bf16[16,32,2]{1,2,0:T(2,128)(2,1)S(1)} all-gather(bf16[1,32,2]{1,2,0:T(2,128)(2,1)S(1)} %bitcast.364), channel_id=1, replica_groups=mesh['dp'=16,'mp'=2] {'dp'}, dimensions={0}, use_global_device_ids=true | all-gather | bytes 2176 | tf_op jit(solution)/shard_map/all_gather | solution.py:248
  176.9 19.3 %all-gather.3 = bf16[16,4,16]{2,1,0:T(4,128)(2,1)S(1)} all-gather(bf16[1,4,16]{2,1,0:T(4,128)(2,1)S(1)} %bitcast.359), channel_id=1, replica_groups=mesh['dp'=16,'mp'=2] {'dp'}, dimensions={0}, use_global_device_ids=true | all-gather | bytes 2176 | tf_op jit(solution)/shard_map/all_gather | solution.py:247
  196.3 66.6 %all-reduce.16.cloned.1.call-done = (f32[1024,512]{1,0:T(8,128)}, f32[1024,512]{1,0:T(8,128)}) async-done(((f32[1024,512]{1,0:T(8,128)}, f32[1024,512]{1,0:T(8,128)}), (f32[1024,512]{1,0:T(8,128)}, f32[1024,512]{1,0:T(8,128)})) %all-reduce.16.cloned.1.call-update) | async-done | bytes 4194320 | tf_op jit(solution)/shard_map/psum | solution.py:85
  262.9 2.8 fusion.154
  267.8 5.3 fusion.149
  273.2 5.7 fusion.163
  280.3 2.3 convolution_convert_fusion.4
  283.5 21.0 %fusion.6 = (bf16[1024,1024]{1,0:T(8,128)(2,1)}, bf16[1024,1024]{1,0:T(8,128)(2,1)}, f32[1024,1024]{1,0:T(8,128)S(1)}) fusion(f32[1024]{0:T(1024)S(1)} %reshape.484, f32[1024,1024]{1,0:T(8,128)S(1)} %copy-done.85, bf16[512,1024]{1,0:T(8,128)(2,1)S(1)} %copy-done.83, f32[1024,512]{1,0:T(8,128)S(1)} %copy-done.5, f32[512]{0:T(512)S(1)} %bitcast.356, ...), kind=kOutput, calls=%fused_computation.20 | convolution fusion | flops 1214775296 | bytes 15745024 | tf_op jit(solution)/shard_map/dot_general | solution.py:12
  304.5 3.8 fusion.164
  309.6 2.3 convolution_convert_fusion.5
  312.0 4.7 convolution_convert_fusion.2
  316.7 4.5 convolution_convert_fusion.3
  321.3 4.3 convolution_convert_fusion
  325.6 4.4 convolution_convert_fusion.1
  330.1 4.2 convolution_convert_fusion.7
  334.3 40.7 %all-reduce.22.cloned.1.call-done = (bf16[1024,512]{1,0:T(8,128)(2,1)}, bf16[1024,512]{1,0:T(8,128)(2,1)}) async-done(((bf16[1024,512]{1,0:T(8,128)(2,1)}, bf16[1024,512]{1,0:T(8,128)(2,1)}), (bf16[1024,512]{1,0:T(8,128)(2,1)}, bf16[1024,512]{1,0:T(8,128)(2,1)})) %all-reduce.22.cloned.1.call-update) | async-done | bytes 2097168 | tf_op jit(solution)/shard_map/psum | solution.py:143
  375.0 3.2 fusion.89
  378.3 6.3 fusion.104
  389.1 16.5 %multiply_reduce_fusion.1 = (f32[4,1024]{1,0:T(4,128)}, f32[4,1024,1024]{1,2,0:T(8,128)}) fusion(f32[4,1024,1024]{1,2,0:T(8,128)} %copy-done, f32[4,1024]{1,0:T(4,128)} %copy-done.49, pred[1024,1024]{0,1:T(8,128)(4,1)S(1)} %get-tuple-element.158, bf16[1024,4,64]{0,2,1:T(8,128)(2,1)} %bitcast.297, bf16[1024,4,64]{0,2,1:T(8,128)(2,1)} %bitcast.311), kind=kOutput, calls=%fused_computation.3 | convolution fusion | flops 557838336 | bytes 35684352 | tf_op jit(solution)/shard_map/qhd,khd->hqk/dot_general | solution.py:161
  405.6 8.3 multiply_convert_fusion.1
  414.0 3.5 fusion.113
  417.5 3.0 bitcast_reduce_fusion.3
  421.0 9.7 bitcast_reduce_fusion
  430.8 12.4 multiply_reduce_fusion
  444.0 12.7 %multiply_convert_fusion = bf16[4,1024,1024]{1,2,0:T(8,128)(2,1)S(1)} fusion(f32[4,1024,1024]{1,2,0:T(8,128)} %get-tuple-element.141, f32[4,1024,1024]{1,2,0:T(8,128)} %copy-done.1, f32[4,1024]{1,0:T(4,128)S(1)} %get-tuple-element.140, f32[4,1024]{1,0:T(4,128)S(1)} %copy-done.52, pred[1024,1024]{0,1:T(8,128)(4,1)S(1)} %copy-done.9), kind=kLoop, calls=%fused_computation | loop fusion | flops 25165824 | bytes 43024384 | tf_op jit(solution)/shard_map/convert_element_type | solution.py:166
  456.7 3.5 fusion.115
  460.2 2.9 bitcast_reduce_fusion.1
  463.2 9.7 bitcast_reduce_fusion.2
  473.9 3.1 convolution_convert_fusion.18
  481.2 3.5 fusion.110
  484.8 2.1 copy.135
  486.9 2.6 copy.137
  491.5 3.0 convolution_convert_fusion.19
  494.6 2.4 fusion.111
  498.5 4.3 convolution_convert_fusion.6
  510.7 44.8 %reduce-scatter.37.cloned.1.call-done = bf16[1024,32]{0,1:T(8,128)(2,1)} async-done(((bf16[1024,512]{0,1:T(8,128)(2,1)}), bf16[1024,32]{0,1:T(8,128)(2,1)}) %reduce-scatter.37.cloned.1.call-update) | async-done | bytes 65552 | tf_op jit(solution)/shard_map/reduce_scatter | solution.py:274
  558.8 57.7 %all-reduce.7 = (bf16[2,4,64]{2,1,0:T(4,128)(2,1)S(1)}, bf16[2,4,64]{2,1,0:T(4,128)(2,1)S(1)}, bf16[16,64]{1,0:T(8,128)(2,1)S(1)}, bf16[16,64]{1,0:T(8,128)(2,1)S(1)}) all-reduce(bf16[2,4,64]{2,1,0:T(4,128)(2,1)S(1)} %pad_maximum_fusion.9, ...), channel_id=11, replica_groups=mesh['dp'=16,'mp'=2] {'dp'}, use_global_device_ids=true, to_apply=%region_43.44.clone | all-reduce | flops 3072 | bytes 12288
  618.6 52.8 %reduce-scatter.41.cloned.1.call-done = bf16[32,2]{1,0:T(8,128)(2,1)} async-done(((bf16[512,2]{1,0:T(8,128)(2,1)}), bf16[32,2]{1,0:T(8,128)(2,1)}) %reduce-scatter.41.cloned.1.call-update) | async-done | bytes 144
  672.8 56.9 %reduce-scatter.31.cloned.1.call-done = bf16[256,32]{0,1:T(8,128)(2,1)} async-done(((bf16[256,512]{0,1:T(8,128)(2,1)}), bf16[256,32]{0,1:T(8,128)(2,1)}) %reduce-scatter.31.cloned.1.call-update) | async-done | bytes 16400 | tf_op jit(solution)/shard_map/reduce_scatter | solution.py:268
  729.7 58.4 %reduce-scatter.29.cloned.1.call-done = bf16[256,32]{0,1:T(8,128)(2,1)} async-done(((bf16[256,512]{0,1:T(8,128)(2,1)}), bf16[256,32]{0,1:T(8,128)(2,1)}) %reduce-scatter.29.cloned.1.call-update) | async-done | bytes 16400 | tf_op jit(solution)/shard_map/reduce_scatter | solution.py:268
  789.4 99.1 %all-reduce.18.cloned.1.call-done = (bf16[3,512,256]{2,0,1:T(4,128)(2,1)}, bf16[3,512,256]{2,0,1:T(4,128)(2,1)}) async-done(((bf16[3,512,256]{2,0,1:T(4,128)(2,1)}, bf16[3,512,256]{2,0,1:T(4,128)(2,1)}), (bf16[3,512,256]{2,0,1:T(4,128)(2,1)}, bf16[3,512,256]{2,0,1:T(4,128)(2,1)})) %all-reduce.18.cloned.1.call-update) | async-done | bytes 1572880
  890.1 108.0 %all-reduce.20.cloned.1.call-done = (bf16[1024,512]{1,0:T(8,128)(2,1)}, bf16[1024,512]{1,0:T(8,128)(2,1)}, bf16[1024,512]{1,0:T(8,128)(2,1)}, bf16[1024,512]{1,0:T(8,128)(2,1)}) async-done(((bf16[1024,512]{1,0:T(8,128)(2,1)}, bf16[1024,512]{1,0:T(8,128)(2,1)}, bf16[1024,512]{1,0:T(8,128)(2,1)}, bf16[1024,512]{1,0:T(8,128)(2,1)}), (bf16[1024,512]{1,0:T(8,128)(2,1)}, bf16[1024,512]{1,0:T(8,128)(2,1)}, ...) | async-done | bytes 4194320 | tf_op jit(solution)/shard_map/psum | solution.py:92
  998.1 3.8 fusion.91
  1003.0 3.3 add_bitcast_fusion.1
  1006.2 2.5 pad_maximum_fusion
  1013.0 4.1 fusion.67
  1017.1 2.5 pad_maximum_fusion.1
  1019.6 39.0 %reduce-scatter.45.cloned.1.call-done = bf16[32,2]{1,0:T(8,128)(2,1)} async-done(((bf16[512,2]{1,0:T(8,128)(2,1)}), bf16[32,2]{1,0:T(8,128)(2,1)}) %reduce-scatter.45.cloned.1.call-update) | async-done | bytes 144
  1059.4 57.4 %reduce-scatter.47.cloned.1.call-done = bf16[32,2]{1,0:T(8,128)(2,1)} async-done(((bf16[512,2]{1,0:T(8,128)(2,1)}), bf16[32,2]{1,0:T(8,128)(2,1)}) %reduce-scatter.47.cloned.1.call-update) | async-done | bytes 144
  1117.6 57.4 %reduce-scatter.49.cloned.1.call-done = bf16[32,2]{1,0:T(8,128)(2,1)} async-done(((bf16[512,2]{1,0:T(8,128)(2,1)}), bf16[32,2]{1,0:T(8,128)(2,1)}) %reduce-scatter.49.cloned.1.call-update) | async-done | bytes 144
  1175.7 57.4 %reduce-scatter.51.cloned.1.call-done = bf16[32,2]{1,0:T(8,128)(2,1)} async-done(((bf16[512,2]{1,0:T(8,128)(2,1)}), bf16[32,2]{1,0:T(8,128)(2,1)}) %reduce-scatter.51.cloned.1.call-update) | async-done | bytes 144
  (337 shorter events, 64.5 us)
Async XLA Ops:
  8.0 85.3 %copy-start.2 = (bf16[2,1024,512]{2,1,0:T(8,128)(2,1)S(1)}, bf16[2,1024,512]{2,1,0:T(8,128)(2,1)}, u32[]{:S(2)}) copy-start(bf16[2,1024,512]{2,1,0:T(8,128)(2,1)} %param.13) | copy-start | bytes 6291460
  8.0 65.6 %copy-start.61 = (bf16[3,32,256]{2,1,0:T(8,128)(2,1)S(1)}, bf16[3,32,256]{2,1,0:T(8,128)(2,1)}, u32[]{:S(2)}) copy-start(bf16[3,32,256]{2,1,0:T(8,128)(2,1)} %param.15) | copy-start | bytes 147460
  8.0 254.9 %all-reduce.16.cloned.1.call-start = ((), (), s32[]{:S(2)}) async-start(), calls=%async_computation.26 | async-start | bytes 8388608 | tf_op jit(solution)/shard_map/psum | solution.py:85
  32.4 61.9 %copy-start.62 = (f32[1,512]{1,0:T(1,128)}, f32[1,512]{1,0:T(1,128)S(1)}, u32[]{:S(2)}) copy-start(f32[1,512]{1,0:T(1,128)S(1)} %get-tuple-element.127) | copy-start | bytes 6148
  50.1 44.2 %copy-start.65 = (f32[1,512]{1,0:T(1,128)}, f32[1,512]{1,0:T(1,128)S(1)}, u32[]{:S(2)}) copy-start(f32[1,512]{1,0:T(1,128)S(1)} %get-tuple-element.129) | copy-start | bytes 6148
  52.0 42.8 %copy-start.53 = (f32[1024]{0:T(1024)}, f32[1024]{0:T(1024)S(1)}, u32[]{:S(2)}) copy-start(f32[1024]{0:T(1024)S(1)} %get-tuple-element.156) | copy-start | bytes 12292
  52.0 42.7 %copy-start.55 = (f32[1024]{0:T(1024)}, f32[1024]{0:T(1024)S(1)}, u32[]{:S(2)}) copy-start(f32[1024]{0:T(1024)S(1)} %get-tuple-element.157) | copy-start | bytes 12292
  54.4 41.6 %copy-start.57 = (f32[1024]{0:T(1024)}, f32[1024]{0:T(1024)S(1)}, u32[]{:S(2)}) copy-start(f32[1024]{0:T(1024)S(1)} %add_rsqrt_fusion.3) | copy-start | bytes 12292
  54.5 41.6 %copy-start.59 = (f32[1024]{0:T(1024)}, f32[1024]{0:T(1024)S(1)}, u32[]{:S(2)}) copy-start(f32[1024]{0:T(1024)S(1)} %add_rsqrt_fusion.1) | copy-start | bytes 12292
  94.8 36.3 %copy-start.19 = (bf16[1024,256]{0,1:T(8,128)(2,1)}, bf16[1024,256]{0,1:T(8,128)(2,1)S(1)}, u32[]{:S(2)}) copy-start(bf16[1024,256]{0,1:T(8,128)(2,1)S(1)} %convolution_convert_fusion.17) | copy-start | bytes 1572868
  99.2 26.1 %copy-start.24 = (bf16[1024,256]{0,1:T(8,128)(2,1)}, bf16[1024,256]{0,1:T(8,128)(2,1)S(1)}, u32[]{:S(2)}) copy-start(bf16[1024,256]{0,1:T(8,128)(2,1)S(1)} %fusion.109) | copy-start | bytes 1572868
  99.7 25.6 %copy-start.17 = (bf16[1024,256]{0,1:T(8,128)(2,1)}, bf16[1024,256]{0,1:T(8,128)(2,1)S(1)}, u32[]{:S(2)}) copy-start(bf16[1024,256]{0,1:T(8,128)(2,1)S(1)} %convolution_convert_fusion.15) | copy-start | bytes 1572868
  119.6 266.8 %copy-start.15 = (bf16[256,512]{0,1:T(8,128)(2,1)}, bf16[256,512]{0,1:T(8,128)(2,1)S(1)}, u32[]{:S(2)}) copy-start(bf16[256,512]{0,1:T(8,128)(2,1)S(1)} %all_gather.40) | copy-start | bytes 786436
  122.0 16.1 %copy-start.8 = (pred[1024,1024]{0,1:T(8,128)(4,1)}, pred[1024,1024]{0,1:T(8,128)(4,1)S(1)}, u32[]{:S(2)}) copy-start(pred[1024,1024]{0,1:T(8,128)(4,1)S(1)} %get-tuple-element.159) | copy-start | bytes 3145732
  134.4 15.9 %copy-start = (f32[4,1024,1024]{1,2,0:T(8,128)}, f32[4,1024,1024]{1,2,0:T(8,128)S(1)}, u32[]{:S(2)}) copy-start(f32[4,1024,1024]{1,2,0:T(8,128)S(1)} %get-tuple-element.138) | copy-start | bytes 50331652
  138.1 12.2 copy-start.49
  138.1 12.2 copy-start.41
  154.9 22.0 %copy-start.78 = (bf16[16,4]{0,1:T(4,128)(2,1)S(1)}, bf16[16,4]{0,1:T(4,128)(2,1)}, u32[]{:S(2)}) copy-start(bf16[16,4]{0,1:T(4,128)(2,1)} %param.20) | copy-start | bytes 388
  157.6 110.2 %all-gather.7.cloned.1.call-start = ((), (), s32[]{:S(2)}) async-start(), calls=%async_computation.12 | async-start | bytes 1114112 | tf_op jit(solution)/shard_map/all_gather | solution.py:244
  158.1 115.0 %all-gather.9.cloned.1.call-start = ((), (), s32[]{:S(2)}) async-start(), calls=%async_computation.13 | async-start | bytes 1114112 | tf_op jit(solution)/shard_map/all_gather | solution.py:245
  158.7 216.3 %all-reduce.22.cloned.1.call-start = ((), (), s32[]{:S(2)}) async-start(), calls=%async_computation.29 | async-start | bytes 4194304 | tf_op jit(solution)/shard_map/psum | solution.py:143
  273.2 7.1 copy-start.83
  283.5 21.0 %copy-start.22 = (bf16[2,1024,512]{2,1,0:T(8,128)(2,1)S(1)}, bf16[2,1024,512]{2,1,0:T(8,128)(2,1)}, u32[]{:S(2)}) copy-start(bf16[2,1024,512]{2,1,0:T(8,128)(2,1)} %param.14) | copy-start | bytes 6291460
  283.5 21.0 %copy-start.82 = (bf16[1024,512]{0,1:T(8,128)(2,1)S(1)}, bf16[1024,512]{0,1:T(8,128)(2,1)}, u32[]{:S(2)}) copy-start(bf16[1024,512]{0,1:T(8,128)(2,1)} %all-gather.9.cloned.1.call-done) | copy-start | bytes 3145732
  311.9 197.2 %reduce-scatter.35.cloned.1.call-start = ((), (), s32[]{:S(2)}) async-start(), calls=%async_computation.17 | async-start | bytes 1114112 | tf_op jit(solution)/shard_map/reduce_scatter | solution.py:271
  316.7 192.5 %reduce-scatter.33.cloned.1.call-start = ((), (), s32[]{:S(2)}) async-start(), calls=%async_computation.16 | async-start | bytes 1114112 | tf_op jit(solution)/shard_map/reduce_scatter | solution.py:271
  321.2 189.5 %reduce-scatter.39.cloned.1.call-start = ((), (), s32[]{:S(2)}) async-start(), calls=%async_computation.19 | async-start | bytes 1114112 | tf_op jit(solution)/shard_map/reduce_scatter | solution.py:274
  325.6 229.9 %reduce-scatter.37.cloned.1.call-start = ((), (), s32[]{:S(2)}) async-start(), calls=%async_computation.18 | async-start | bytes 1114112 | tf_op jit(solution)/shard_map/reduce_scatter | solution.py:274
  330.0 287.8 %reduce-scatter.43.cloned.1.call-start = ((), (), s32[]{:S(2)}) async-start(), calls=%async_computation.21 | async-start | bytes 139264
  389.1 16.5 %slice-start = ((s8[16777216]{0:T(1024)(128)(4,1)}), s8[4194304]{0:T(1024)(128)(4,1)S(1)}, s32[]{:S(2)}) async-start(s8[16777216]{0:T(1024)(128)(4,1)} %bitcast.287), calls=%async_computation.30 | async-start | bytes 8388608
  389.1 16.5 %slice-start.1 = ((s8[16777216]{0:T(1024)(128)(4,1)}), s8[4194304]{0:T(1024)(128)(4,1)S(1)}, s32[]{:S(2)}) async-start(s8[16777216]{0:T(1024)(128)(4,1)} %bitcast.287), calls=%async_computation.31 | async-start | bytes 8388608
  389.1 16.5 %slice-start.2 = ((s8[16777216]{0:T(1024)(128)(4,1)}), s8[4194304]{0:T(1024)(128)(4,1)S(1)}, s32[]{:S(2)}) async-start(s8[16777216]{0:T(1024)(128)(4,1)} %bitcast.287), calls=%async_computation.32 | async-start | bytes 8388608
  389.1 16.5 %slice-start.3 = ((s8[16777216]{0:T(1024)(128)(4,1)}), s8[4194304]{0:T(1024)(128)(4,1)S(1)}, s32[]{:S(2)}) async-start(s8[16777216]{0:T(1024)(128)(4,1)} %bitcast.287), calls=%async_computation.33 | async-start | bytes 8388608
  405.6 8.4 copy-start.27
  421.0 9.7 copy-start.40
  430.8 12.4 copy-start.72
  430.8 12.4 copy-start.71
  430.8 13.3 %copy-start.75 = (bf16[512]{0:T(512)(128)(2,1)S(1)}, bf16[512]{0:T(512)(128)(2,1)}, u32[]{:S(2)}) copy-start(bf16[512]{0:T(512)(128)(2,1)} %get-tuple-element.102) | copy-start | bytes 3076
  444.0 12.7 %copy-start.25 = (bf16[1024,256]{0,1:T(8,128)(2,1)S(1)}, bf16[1024,256]{0,1:T(8,128)(2,1)}, u32[]{:S(2)}) copy-start(bf16[1024,256]{0,1:T(8,128)(2,1)} %copy-done.24) | copy-start | bytes 1572868
  472.9 7.2 copy-start.32
  472.9 8.3 copy-start.3
  472.9 8.3 copy-start.56
  472.9 8.3 copy-start.58
  472.9 8.3 copy-start.63
  472.9 8.3 copy-start.66
  473.0 198.5 %reduce-scatter.41.cloned.1.call-start = ((), (), s32[]{:S(2)}) async-start(), calls=%async_computation.20 | async-start | bytes 139264
  473.9 255.8 %reduce-scatter.31.cloned.1.call-start = ((), (), s32[]{:S(2)}) async-start(), calls=%async_computation.15 | async-start | bytes 278528 | tf_op jit(solution)/shard_map/reduce_scatter | solution.py:268
  481.1 8.3 copy-start.35
  481.1 306.9 %reduce-scatter.29.cloned.1.call-start = ((), (), s32[]{:S(2)}) async-start(), calls=%async_computation.14 | async-start | bytes 278528 | tf_op jit(solution)/shard_map/reduce_scatter | solution.py:268
  484.8 9.8 copy-start.54
  484.8 9.8 copy-start.60
  494.5 394.0 %all-reduce.18.cloned.1.call-start = ((), (), s32[]{:S(2)}) async-start(), calls=%async_computation.27 | async-start | bytes 4194304
  498.4 499.7 %all-reduce.20.cloned.1.call-start = ((), (), s32[]{:S(2)}) async-start(), calls=%async_computation.28 | async-start | bytes 8388608 | tf_op jit(solution)/shard_map/psum | solution.py:92
  504.9 52.1 %copy-start.12 = (bf16[1024,512]{1,0:T(8,128)(2,1)S(1)}, bf16[1024,512]{1,0:T(8,128)(2,1)}, u32[]{:S(2)}) copy-start(bf16[1024,512]{1,0:T(8,128)(2,1)} %get-tuple-element.100) | copy-start | bytes 3145732
  507.0 51.7 %copy-start.70 = (bf16[512]{0:T(512)(128)(2,1)S(1)}, bf16[512]{0:T(512)(128)(2,1)}, u32[]{:S(2)}) copy-start(bf16[512]{0:T(512)(128)(2,1)} %get-tuple-element.132) | copy-start | bytes 3076
  507.0 51.7 %copy-start.73 = (bf16[4,64]{1,0:T(4,128)(2,1)S(1)}, bf16[4,64]{1,0:T(4,128)(2,1)}, u32[]{:S(2)}) copy-start(bf16[4,64]{1,0:T(4,128)(2,1)} %get-tuple-element.150) | copy-start | bytes 1540
  507.0 51.7 %copy-start.80 = (bf16[4,64]{1,0:T(4,128)(2,1)S(1)}, bf16[4,64]{1,0:T(4,128)(2,1)}, u32[]{:S(2)}) copy-start(bf16[4,64]{1,0:T(4,128)(2,1)} %get-tuple-element.148) | copy-start | bytes 1540
  507.0 51.8 %copy-start.74 = (bf16[4,64]{1,0:T(4,128)(2,1)S(1)}, bf16[4,64]{1,0:T(4,128)(2,1)}, u32[]{:S(2)}) copy-start(bf16[4,64]{1,0:T(4,128)(2,1)} %get-tuple-element.146) | copy-start | bytes 1540
  507.0 51.8 %copy-start.79 = (bf16[4,64]{1,0:T(4,128)(2,1)S(1)}, bf16[4,64]{1,0:T(4,128)(2,1)}, u32[]{:S(2)}) copy-start(bf16[4,64]{1,0:T(4,128)(2,1)} %get-tuple-element.144) | copy-start | bytes 1540
  507.0 495.9 %copy-start.69 = (f32[1,512]{1,0:T(1,128)S(1)}, f32[1,512]{1,0:T(1,128)}, u32[]{:S(2)}) copy-start(f32[1,512]{1,0:T(1,128)} %get-tuple-element.122) | copy-start | bytes 6148
  507.0 551.6 %reduce-scatter.45.cloned.1.call-start = ((), (), s32[]{:S(2)}) async-start(), calls=%async_computation.22 | async-start | bytes 139264
  1002.9 113.9 %reduce-scatter.47.cloned.1.call-start = ((), (), s32[]{:S(2)}) async-start(), calls=%async_computation.23 | async-start | bytes 139264
  1011.0 163.9 %reduce-scatter.49.cloned.1.call-start = ((), (), s32[]{:S(2)}) async-start(), calls=%async_computation.24 | async-start | bytes 139264
  1012.1 221.0 %reduce-scatter.51.cloned.1.call-start = ((), (), s32[]{:S(2)}) async-start(), calls=%async_computation.25 | async-start | bytes 139264
  (46 other events, 172.2 us)
Sparse Core Ops, SparseCore 0:
  157.7 105.1 all-reduce.15
  312.0 62.9 all-reduce.21
Sparse Core Ops, SparseCore 1:
  160.2 35.0 all-gather.6
  197.3 36.8 all-gather.8
  316.8 57.6 reduce-scatter.34
  378.1 56.6 reduce-scatter.32
  438.4 56.7 reduce-scatter.38
  498.8 56.6 reduce-scatter.36
  558.8 54.6 reduce-scatter.42
  616.8 54.6 reduce-scatter.40
  674.8 54.8 reduce-scatter.30
  733.2 54.8 reduce-scatter.28
  791.5 96.9 all-reduce.17
  891.1 107.0 all-reduce.19
  1003.0 55.6 reduce-scatter.44
  1062.1 54.6 reduce-scatter.46
  1120.3 54.6 reduce-scatter.48
  1178.4 54.7 reduce-scatter.50
where the time goes:
time: 1250 us; the launch traced here: 1240 us
  waiting for transfers between devices  740 us (59%)
  blocking collectives  193 us (15%)
  matrix products  176 us (14%)
  other arithmetic  78.4 us (6%)
  local copies, waits for them, and re-layouts  35.5 us (3%)
  between operations  18.9 us (2%)
    unnamed x25, waiting for transfers between devices  364 us
    reduce_scatter x2, waiting for transfers between devices, body(): lax.psum_scatter(local_grads[1].astype(jnp.bfloat16), 'dp', scatter_dimen...  115 us
    psum x1, waiting for transfers between devices, forward(): lax.psum(partial_ffn.astype(jnp.bfloat16), 'mp').astype(jnp.float32)  108 us
    dot_general x24, matrix products, product(): return jnp.dot(left, right, preferred_element_type=jnp.float32)  83.6 us
    psum x1, waiting for transfers between devices, forward(): resid = rows_in + lax.psum(partial_attn, 'mp') + bias_out[0]  66.6 us
    unnamed x1, blocking collectives  57.7 us
    reduce_scatter x2, waiting for transfers between devices, body(): lax.psum_scatter(local_grads[3].astype(jnp.bfloat16), 'dp', scatter_dimen...  44.8 us
    psum x1, waiting for transfers between devices, backward(): lax.psum(partial_two.astype(jnp.bfloat16), 'mp').astype(jnp.float32)  40.7 us
  transfers between devices with their start and end apart: 18, of which 12 were waited for; matrix products, arithmetic and copies ran while one was open for 15% of the time, Pallas kernels for 0%

commit v1 on v0

--- a/solution.py
+++ b/solution.py
@@ -1,11 +1,21 @@
+import functools
 import math
 import jax
 import jax.numpy as jnp
 from jax import lax
 from jax.sharding import PartitionSpec as P
+from jax.lax import all_gather
 
 epsilon = 1e-05
 masked_value = -1e30
+
+
+def roots_work(view, axis_name):
+    current_block = all_gather(view, axis_name)
+    return jnp.sum(current_block, axis=0)
+
+
+fix_rates = functools.partial(roots_work, axis_name="mp")
 
 
 def product(left, right):
@@ -88,9 +98,7 @@
     pre = product(hidden_two, up_full) + bias_up.astype(jnp.float32).reshape(-1)
     act = jax.nn.gelu(pre, approximate=False).astype(jnp.bfloat16)
     partial_ffn = product(act, down_full)
-    result = (
-        resid + lax.psum(partial_ffn.astype(jnp.bfloat16), "mp").astype(jnp.float32) + bias_out[1]
-    )
+    result = resid + fix_rates(partial_ffn.astype(jnp.bfloat16)).astype(jnp.float32) + bias_out[1]
     kept = (
         allowed,
         scaled_one,

time: 1250 us -> 1210 us (0.968)
  waiting for transfers between devices: 740 us -> 690 us
    all_gather x0 -> x2, waiting for transfers between devices: none -> 62.9 us  [roots_work(): current_block = all_gather(view, axis_name)]
    psum x1, waiting for transfers between devices: 108 us -> 62.9 us  [backward(): lax.psum(partial_one.astype(jnp.bfloat16), 'mp').astype(jnp.float32)]
    reduce_scatter x2, waiting for transfers between devices: 44.8 us -> 0.01 us  [body(): lax.psum_scatter(local_grads[3].astype(jnp.bfloat16), 'dp', scatter_dimen...]
    unnamed x25 -> x27, waiting for transfers between devices: 364 us -> 345 us
  transfers between devices with their start and end apart: 18 -> 20, of which waited for: 12 -> 13; matrix products, arithmetic and copies ran while one was open for 15% -> 17% of each run, Pallas kernels for 0% -> 0%
where the time goes in v1:
time: 1210 us
  waiting for transfers between devices  690 us (57%)
  blocking collectives  197 us (16%)
  matrix products  178 us (15%)
  other arithmetic  86.4 us (7%)
  local copies, waits for them, and re-layouts  35.7 us (3%)
  between operations  18.4 us (2%)
    unnamed x27, waiting for transfers between devices  345 us
    reduce_scatter x2, waiting for transfers between devices, body(): lax.psum_scatter(local_grads[1].astype(jnp.bfloat16), 'dp', scatter_dimen...  115 us
    dot_general x24, matrix products, product(): return jnp.dot(left, right, preferred_element_type=jnp.float32)  83.2 us
    psum x1, waiting for transfers between devices, forward(): resid = rows_in + lax.psum(partial_attn, 'mp') + bias_out[0]  67.4 us
    all_gather x2, waiting for transfers between devices, roots_work(): current_block = all_gather(view, axis_name)  62.9 us
    psum x1, waiting for transfers between devices, backward(): lax.psum(partial_one.astype(jnp.bfloat16), 'mp').astype(jnp.float32)  62.9 us
    unnamed x1, blocking collectives  61.2 us
    psum x1, waiting for transfers between devices, backward(): lax.psum(partial_two.astype(jnp.bfloat16), 'mp').astype(jnp.float32)  36.3 us
  transfers between devices with their start and end apart: 20, of which 13 were waited for; matrix products, arithmetic and copies ran while one was open for 17% of the time, Pallas kernels for 0%

profile of v1, /device:TPU:0, one launch (start us, length us, event | category | flops | bytes accessed | tf_op | source)
XLA Modules:
  0.0 1206.2 jit_solution(2706881742712626171)
XLA Ops:
  9.0 23.3 %all-gather.2 = bf16[16,32,2]{1,2,0:T(2,128)(2,1)S(1)} all-gather(bf16[1,32,2]{1,2,0:T(2,128)(2,1)} %bitcast.367), channel_id=1, replica_groups=mesh['dp'=16,'mp'=2] {'dp'}, dimensions={0}, use_global_device_ids=true | all-gather | bytes 2176 | tf_op jit(solution)/shard_map/all_gather | solution.py:257
  32.4 17.6 %all-gather.3 = bf16[16,32,2]{1,2,0:T(2,128)(2,1)S(1)} all-gather(bf16[1,32,2]{1,2,0:T(2,128)(2,1)} %bitcast.368), channel_id=1, replica_groups=mesh['dp'=16,'mp'=2] {'dp'}, dimensions={0}, use_global_device_ids=true | all-gather | bytes 2176 | tf_op jit(solution)/shard_map/all_gather | solution.py:258
  54.5 18.8 %all_gather.51 = bf16[2,4,64]{1,0,2:T(2,128)(2,1)S(1)} all-gather(bf16[2,4,4]{1,0,2:T(2,128)(2,1)S(1)} %copy.117), channel_id=1, replica_groups=mesh['dp'=16,'mp'=2] {'dp'}, dimensions={2}, use_global_device_ids=true | all-gather | bytes 1088 | tf_op jit(solution)/shard_map/all_gather | solution.py:254
  73.7 19.6 %all_gather.50 = bf16[3,512,256]{2,1,0:T(8,128)(2,1)S(1)} all-gather(bf16[3,32,256]{2,1,0:T(8,128)(2,1)S(1)} %copy-done.57), channel_id=1, replica_groups=mesh['dp'=16,'mp'=2] {'dp'}, dimensions={1}, use_global_device_ids=true | all-gather | bytes 835584 | tf_op jit(solution)/shard_map/all_gather | solution.py:250
  99.8 20.0 %all_gather.52 = bf16[256,512]{0,1:T(8,128)(2,1)S(1)} all-gather(bf16[256,32]{0,1:T(8,128)(2,1)S(1)} %copy-done.60), channel_id=1, replica_groups=mesh['dp'=16,'mp'=2] {'dp'}, dimensions={1}, use_global_device_ids=true | all-gather | bytes 278528 | tf_op jit(solution)/shard_map/all_gather | solution.py:251
  119.8 2.4 fusion.36
  122.2 3.3 fusion.1
  125.6 3.7 exponential_reduce_fusion
  131.3 3.3 fusion
  134.6 3.7 exponential_reduce_fusion.1
  138.4 10.3 convolution_convert_fusion.14
  150.5 4.6 convolution_convert_fusion.16
  159.0 17.5 %all-gather.4 = bf16[16,32,2]{1,2,0:T(2,128)(2,1)S(1)} all-gather(bf16[1,32,2]{1,2,0:T(2,128)(2,1)S(1)} %bitcast.369), channel_id=1, replica_groups=mesh['dp'=16,'mp'=2] {'dp'}, dimensions={0}, use_global_device_ids=true | all-gather | bytes 2176 | tf_op jit(solution)/shard_map/all_gather | solution.py:256
  176.6 19.0 %all-gather.5 = bf16[16,4,16]{2,1,0:T(4,128)(2,1)S(1)} all-gather(bf16[1,4,16]{2,1,0:T(4,128)(2,1)S(1)} %bitcast.364), channel_id=1, replica_groups=mesh['dp'=16,'mp'=2] {'dp'}, dimensions={0}, use_global_device_ids=true | all-gather | bytes 2176 | tf_op jit(solution)/shard_map/all_gather | solution.py:255
  195.7 67.4 %all-reduce.16.cloned.1.call-done = (f32[1024,512]{1,0:T(8,128)}, f32[1024,512]{1,0:T(8,128)}) async-done(((f32[1024,512]{1,0:T(8,128)}, f32[1024,512]{1,0:T(8,128)}), (f32[1024,512]{1,0:T(8,128)}, f32[1024,512]{1,0:T(8,128)})) %all-reduce.16.cloned.1.call-update) | async-done | bytes 4194320 | tf_op jit(solution)/shard_map/psum | solution.py:95
  263.1 2.8 fusion.154
  268.0 5.3 fusion.149
  273.4 5.7 fusion.163
  283.6 21.0 %fusion.6 = (bf16[1024,1024]{1,0:T(8,128)(2,1)}, bf16[1024,1024]{1,0:T(8,128)(2,1)}, f32[1024,1024]{1,0:T(8,128)S(1)}) fusion(f32[1024]{0:T(1024)S(1)} %reshape.484, f32[1024,1024]{1,0:T(8,128)S(1)} %copy-done.79, bf16[512,1024]{1,0:T(8,128)(2,1)S(1)} %copy-done.77, f32[1024,512]{1,0:T(8,128)S(1)} %copy-done.7, f32[512]{0:T(512)S(1)} %bitcast.361, ...), kind=kOutput, calls=%fused_computation.20 | convolution fusion | flops 1214775296 | bytes 15745024 | tf_op jit(solution)/shard_map/dot_general | solution.py:22
  304.6 3.8 fusion.164
  312.0 4.2 convolution_convert_fusion.6
  316.2 4.7 convolution_convert_fusion.7
  321.2 4.6 convolution_convert_fusion.2
  325.9 4.1 convolution_convert_fusion.3
  330.1 4.3 convolution_convert_fusion
  334.4 4.2 convolution_convert_fusion.1
  338.7 36.3 %all-reduce.22.cloned.1.call-done = (bf16[1024,512]{1,0:T(8,128)(2,1)}, bf16[1024,512]{1,0:T(8,128)(2,1)}) async-done(((bf16[1024,512]{1,0:T(8,128)(2,1)}, bf16[1024,512]{1,0:T(8,128)(2,1)}), (bf16[1024,512]{1,0:T(8,128)(2,1)}, bf16[1024,512]{1,0:T(8,128)(2,1)})) %all-reduce.22.cloned.1.call-update) | async-done | bytes 2097168 | tf_op jit(solution)/shard_map/psum | solution.py:151
  375.1 3.1 fusion.89
  378.2 31.6 %all-gather.17.cloned.1.call-done = bf16[2048,512]{1,0:T(8,128)(2,1)} async-done(((bf16[1024,512]{1,0:T(8,128)(2,1)}), bf16[2048,512]{1,0:T(8,128)(2,1)}) %all-gather.17.cloned.1.call-update) | async-done | bytes 2097168 | tf_op jit(solution)/shard_map/all_gather | solution.py:14
  409.8 3.2 reduce_sum.383
  413.0 31.3 %all-gather.15.cloned.1.call-done = bf16[2048,512]{1,0:T(8,128)(2,1)} async-done(((bf16[1024,512]{1,0:T(8,128)(2,1)}), bf16[2048,512]{1,0:T(8,128)(2,1)}) %all-gather.15.cloned.1.call-update) | async-done | bytes 2097168 | tf_op jit(solution)/shard_map/all_gather | solution.py:14
  444.3 3.2 reduce_sum.377
  447.5 7.9 fusion.104
  455.5 2.8 fusion.150
  460.9 16.2 %multiply_reduce_fusion.1 = (f32[4,1024]{1,0:T(4,128)}, f32[4,1024,1024]{1,2,0:T(8,128)}) fusion(f32[4,1024,1024]{1,2,0:T(8,128)} %copy-done, f32[4,1024]{1,0:T(4,128)} %copy-done.45, pred[1024,1024]{0,1:T(8,128)(4,1)S(1)} %get-tuple-element.156, bf16[1024,4,64]{0,2,1:T(8,128)(2,1)} %bitcast.299, bf16[1024,4,64]{0,2,1:T(8,128)(2,1)} %bitcast.315), kind=kOutput, calls=%fused_computation.3 | convolution fusion | flops 557838336 | bytes 35684352 | tf_op jit(solution)/shard_map/qhd,khd->hqk/dot_general | solution.py:169
  477.2 8.4 multiply_convert_fusion.1
  485.7 3.5 fusion.113
  489.2 3.0 bitcast_reduce_fusion.3
  492.6 9.7 bitcast_reduce_fusion
  502.4 12.3 %multiply_reduce_fusion = (f32[4,1024]{1,0:T(4,128)S(1)}, f32[4,1024,1024]{1,2,0:T(8,128)}) fusion(f32[4,1024,1024]{1,2,0:T(8,128)} %copy-done.1, f32[4,1024]{1,0:T(4,128)S(1)} %copy-done.48, pred[1024,1024]{0,1:T(8,128)(4,1)S(1)} %copy-done.5, bf16[1024,4,64]{0,2,1:T(8,128)(2,1)S(1)} %bitcast.302, bf16[1024,4,64]{0,2,1:T(8,128)(2,1)S(1)} %bitcast.314), kind=kOutput, calls=%fused_computation.1 | convolution fusion | flops 557838336 | bytes 35684352 | tf_op jit(solution)/shard_map/qhd,khd->hqk/dot_general | solution.py:169
  515.6 12.6 %multiply_convert_fusion = bf16[4,1024,1024]{1,2,0:T(8,128)(2,1)S(1)} fusion(f32[4,1024,1024]{1,2,0:T(8,128)} %get-tuple-element.139, f32[4,1024,1024]{1,2,0:T(8,128)} %copy-done.1, f32[4,1024]{1,0:T(4,128)S(1)} %get-tuple-element.138, f32[4,1024]{1,0:T(4,128)S(1)} %copy-done.48, pred[1024,1024]{0,1:T(8,128)(4,1)S(1)} %copy-done.5), kind=kLoop, calls=%fused_computation | loop fusion | flops 25165824 | bytes 43024384 | tf_op jit(solution)/shard_map/convert_element_type | solution.py:174
  528.2 3.5 fusion.115
  531.7 2.9 bitcast_reduce_fusion.1
  534.6 9.6 bitcast_reduce_fusion.2
  545.3 3.0 convolution_convert_fusion.18
  552.5 3.5 fusion.110
  558.1 2.5 copy.137
  562.7 3.0 convolution_convert_fusion.19
  565.8 3.5 fusion.111
  571.8 3.4 bitcast_convert_fusion.1
  584.3 61.2 %all-reduce.7 = (bf16[2,4,64]{2,1,0:T(4,128)(2,1)S(1)}, bf16[2,4,64]{2,1,0:T(4,128)(2,1)S(1)}, bf16[16,64]{1,0:T(8,128)(2,1)S(1)}, bf16[16,64]{1,0:T(8,128)(2,1)S(1)}) all-reduce(bf16[2,4,64]{2,1,0:T(4,128)(2,1)S(1)} %pad_maximum_fusion.9, ...), channel_id=13, replica_groups=mesh['dp'=16,'mp'=2] {'dp'}, use_global_device_ids=true, to_apply=%region_43.44.clone | all-reduce | flops 3072 | bytes 12288
  646.9 4.7 pad_maximum_fusion
  652.3 27.9 %reduce-scatter.43.cloned.1.call-done = bf16[32,2]{1,0:T(8,128)(2,1)} async-done(((bf16[512,2]{1,0:T(8,128)(2,1)}), bf16[32,2]{1,0:T(8,128)(2,1)}) %reduce-scatter.43.cloned.1.call-update) | async-done | bytes 144
  681.6 56.9 %reduce-scatter.31.cloned.1.call-done = bf16[256,32]{0,1:T(8,128)(2,1)} async-done(((bf16[256,512]{0,1:T(8,128)(2,1)}), bf16[256,32]{0,1:T(8,128)(2,1)}) %reduce-scatter.31.cloned.1.call-update) | async-done | bytes 16400 | tf_op jit(solution)/shard_map/reduce_scatter | solution.py:276
  738.5 58.3 %reduce-scatter.29.cloned.1.call-done = bf16[256,32]{0,1:T(8,128)(2,1)} async-done(((bf16[256,512]{0,1:T(8,128)(2,1)}), bf16[256,32]{0,1:T(8,128)(2,1)}) %reduce-scatter.29.cloned.1.call-update) | async-done | bytes 16400 | tf_op jit(solution)/shard_map/reduce_scatter | solution.py:276
  798.2 99.0 %all-reduce.18.cloned.1.call-done = (bf16[3,512,256]{2,0,1:T(4,128)(2,1)}, bf16[3,512,256]{2,0,1:T(4,128)(2,1)}) async-done(((bf16[3,512,256]{2,0,1:T(4,128)(2,1)}, bf16[3,512,256]{2,0,1:T(4,128)(2,1)}), (bf16[3,512,256]{2,0,1:T(4,128)(2,1)}, bf16[3,512,256]{2,0,1:T(4,128)(2,1)})) %all-reduce.18.cloned.1.call-update) | async-done | bytes 1572880
  898.8 62.9 %all-reduce.20.cloned.1.call-done = (bf16[1024,512]{1,0:T(8,128)(2,1)}, bf16[1024,512]{1,0:T(8,128)(2,1)}) async-done(((bf16[1024,512]{1,0:T(8,128)(2,1)}, bf16[1024,512]{1,0:T(8,128)(2,1)}), (bf16[1024,512]{1,0:T(8,128)(2,1)}, bf16[1024,512]{1,0:T(8,128)(2,1)})) %all-reduce.20.cloned.1.call-update) | async-done | bytes 2097168 | tf_op jit(solution)/shard_map/psum | solution.py:195
  961.7 3.8 fusion.91
  970.8 4.1 fusion.67
  975.0 2.5 pad_maximum_fusion.1
  977.4 44.8 %reduce-scatter.45.cloned.1.call-done = bf16[32,2]{1,0:T(8,128)(2,1)} async-done(((bf16[512,2]{1,0:T(8,128)(2,1)}), bf16[32,2]{1,0:T(8,128)(2,1)}) %reduce-scatter.45.cloned.1.call-update) | async-done | bytes 144
  1022.9 57.4 %reduce-scatter.47.cloned.1.call-done = bf16[32,2]{1,0:T(8,128)(2,1)} async-done(((bf16[512,2]{1,0:T(8,128)(2,1)}), bf16[32,2]{1,0:T(8,128)(2,1)}) %reduce-scatter.47.cloned.1.call-update) | async-done | bytes 144
  1081.1 57.4 %reduce-scatter.49.cloned.1.call-done = bf16[32,2]{1,0:T(8,128)(2,1)} async-done(((bf16[512,2]{1,0:T(8,128)(2,1)}), bf16[32,2]{1,0:T(8,128)(2,1)}) %reduce-scatter.49.cloned.1.call-update) | async-done | bytes 144
  1139.3 57.4 %reduce-scatter.51.cloned.1.call-done = bf16[32,2]{1,0:T(8,128)(2,1)} async-done(((bf16[512,2]{1,0:T(8,128)(2,1)}), bf16[32,2]{1,0:T(8,128)(2,1)}) %reduce-scatter.51.cloned.1.call-update) | async-done | bytes 144
  (333 shorter events, 70.3 us)
Async XLA Ops:
  8.0 85.3 %copy-start.2 = (bf16[2,1024,512]{2,1,0:T(8,128)(2,1)S(1)}, bf16[2,1024,512]{2,1,0:T(8,128)(2,1)}, u32[]{:S(2)}) copy-start(bf16[2,1024,512]{2,1,0:T(8,128)(2,1)} %param.13) | copy-start | bytes 6291460
  8.0 65.6 %copy-start.57 = (bf16[3,32,256]{2,1,0:T(8,128)(2,1)S(1)}, bf16[3,32,256]{2,1,0:T(8,128)(2,1)}, u32[]{:S(2)}) copy-start(bf16[3,32,256]{2,1,0:T(8,128)(2,1)} %param.15) | copy-start | bytes 147460
  8.0 255.1 %all-reduce.16.cloned.1.call-start = ((), (), s32[]{:S(2)}) async-start(), calls=%async_computation.28 | async-start | bytes 8388608 | tf_op jit(solution)/shard_map/psum | solution.py:95
  32.4 61.9 %copy-start.58 = (f32[1,512]{1,0:T(1,128)}, f32[1,512]{1,0:T(1,128)S(1)}, u32[]{:S(2)}) copy-start(f32[1,512]{1,0:T(1,128)S(1)} %get-tuple-element.127) | copy-start | bytes 6148
  50.1 44.2 %copy-start.61 = (f32[1,512]{1,0:T(1,128)}, f32[1,512]{1,0:T(1,128)S(1)}, u32[]{:S(2)}) copy-start(f32[1,512]{1,0:T(1,128)S(1)} %get-tuple-element.129) | copy-start | bytes 6148
  52.0 42.7 %copy-start.49 = (f32[1024]{0:T(1024)}, f32[1024]{0:T(1024)S(1)}, u32[]{:S(2)}) copy-start(f32[1024]{0:T(1024)S(1)} %get-tuple-element.154) | copy-start | bytes 12292
  52.0 42.7 %copy-start.51 = (f32[1024]{0:T(1024)}, f32[1024]{0:T(1024)S(1)}, u32[]{:S(2)}) copy-start(f32[1024]{0:T(1024)S(1)} %get-tuple-element.155) | copy-start | bytes 12292
  54.4 41.6 %copy-start.53 = (f32[1024]{0:T(1024)}, f32[1024]{0:T(1024)S(1)}, u32[]{:S(2)}) copy-start(f32[1024]{0:T(1024)S(1)} %add_rsqrt_fusion.3) | copy-start | bytes 12292
  54.5 41.6 %copy-start.55 = (f32[1024]{0:T(1024)}, f32[1024]{0:T(1024)S(1)}, u32[]{:S(2)}) copy-start(f32[1024]{0:T(1024)S(1)} %add_rsqrt_fusion.1) | copy-start | bytes 12292
  94.8 36.5 %copy-start.18 = (bf16[1024,256]{0,1:T(8,128)(2,1)}, bf16[1024,256]{0,1:T(8,128)(2,1)S(1)}, u32[]{:S(2)}) copy-start(bf16[1024,256]{0,1:T(8,128)(2,1)S(1)} %convolution_convert_fusion.17) | copy-start | bytes 1572868
  99.2 26.3 %copy-start.24 = (bf16[1024,256]{0,1:T(8,128)(2,1)}, bf16[1024,256]{0,1:T(8,128)(2,1)S(1)}, u32[]{:S(2)}) copy-start(bf16[1024,256]{0,1:T(8,128)(2,1)S(1)} %fusion.109) | copy-start | bytes 1572868
  99.7 25.8 %copy-start.16 = (bf16[1024,256]{0,1:T(8,128)(2,1)}, bf16[1024,256]{0,1:T(8,128)(2,1)S(1)}, u32[]{:S(2)}) copy-start(bf16[1024,256]{0,1:T(8,128)(2,1)S(1)} %convolution_convert_fusion.15) | copy-start | bytes 1572868
  119.8 338.5 %copy-start.14 = (bf16[256,512]{0,1:T(8,128)(2,1)}, bf16[256,512]{0,1:T(8,128)(2,1)S(1)}, u32[]{:S(2)}) copy-start(bf16[256,512]{0,1:T(8,128)(2,1)S(1)} %all_gather.52) | copy-start | bytes 786436
  122.2 16.1 %copy-start.4 = (pred[1024,1024]{0,1:T(8,128)(4,1)}, pred[1024,1024]{0,1:T(8,128)(4,1)S(1)}, u32[]{:S(2)}) copy-start(pred[1024,1024]{0,1:T(8,128)(4,1)S(1)} %get-tuple-element.157) | copy-start | bytes 3145732
  131.3 7.0 copy-start.47
  134.6 15.9 %copy-start = (f32[4,1024,1024]{1,2,0:T(8,128)}, f32[4,1024,1024]{1,2,0:T(8,128)S(1)}, u32[]{:S(2)}) copy-start(f32[4,1024,1024]{1,2,0:T(8,128)S(1)} %get-tuple-element.136) | copy-start | bytes 50331652
  138.3 12.2 %copy-start.45 = (f32[4,1024]{1,0:T(4,128)}, f32[4,1024]{1,0:T(4,128)S(1)}, u32[]{:S(2)}) copy-start(f32[4,1024]{1,0:T(4,128)S(1)} %log_add_fusion.1) | copy-start | bytes 49156
  138.4 12.2 %copy-start.40 = (bf16[1024,256]{0,1:T(8,128)(2,1)S(1)}, bf16[1024,256]{0,1:T(8,128)(2,1)}, u32[]{:S(2)}) copy-start(bf16[1024,256]{0,1:T(8,128)(2,1)} %fusion.106) | copy-start | bytes 1572868
  155.2 21.4 %copy-start.72 = (bf16[16,4]{0,1:T(4,128)(2,1)S(1)}, bf16[16,4]{0,1:T(4,128)(2,1)}, u32[]{:S(2)}) copy-start(bf16[16,4]{0,1:T(4,128)(2,1)} %param.20) | copy-start | bytes 388
  157.8 110.2 %all-gather.11.cloned.1.call-start = ((), (), s32[]{:S(2)}) async-start(), calls=%async_computation.12 | async-start | bytes 1114112 | tf_op jit(solution)/shard_map/all_gather | solution.py:252
  158.4 115.0 %all-gather.13.cloned.1.call-start = ((), (), s32[]{:S(2)}) async-start(), calls=%async_computation.13 | async-start | bytes 1114112 | tf_op jit(solution)/shard_map/all_gather | solution.py:253
  159.0 216.1 %all-reduce.22.cloned.1.call-start = ((), (), s32[]{:S(2)}) async-start(), calls=%async_computation.31 | async-start | bytes 4194304 | tf_op jit(solution)/shard_map/psum | solution.py:151
  273.4 7.0 copy-start.77
  283.6 21.0 %copy-start.21 = (bf16[2,1024,512]{2,1,0:T(8,128)(2,1)S(1)}, bf16[2,1024,512]{2,1,0:T(8,128)(2,1)}, u32[]{:S(2)}) copy-start(bf16[2,1024,512]{2,1,0:T(8,128)(2,1)} %param.14) | copy-start | bytes 6291460
  283.6 21.0 %copy-start.76 = (bf16[1024,512]{0,1:T(8,128)(2,1)S(1)}, bf16[1024,512]{0,1:T(8,128)(2,1)}, u32[]{:S(2)}) copy-start(bf16[1024,512]{0,1:T(8,128)(2,1)} %all-gather.13.cloned.1.call-done) | copy-start | bytes 3145732
  311.9 97.8 %all-gather.17.cloned.1.call-start = ((), (), s32[]{:S(2)}) async-start(), calls=%async_computation.21 | async-start | bytes 3145728 | tf_op jit(solution)/shard_map/all_gather | solution.py:14
  316.2 128.1 %all-gather.15.cloned.1.call-start = ((), (), s32[]{:S(2)}) async-start(), calls=%async_computation.20 | async-start | bytes 3145728 | tf_op jit(solution)/shard_map/all_gather | solution.py:14
  320.9 258.5 %reduce-scatter.35.cloned.1.call-start = ((), (), s32[]{:S(2)}) async-start(), calls=%async_computation.17 | async-start | bytes 1114112 | tf_op jit(solution)/shard_map/reduce_scatter | solution.py:279
  325.8 253.6 %reduce-scatter.33.cloned.1.call-start = ((), (), s32[]{:S(2)}) async-start(), calls=%async_computation.16 | async-start | bytes 1114112 | tf_op jit(solution)/shard_map/reduce_scatter | solution.py:279
  330.0 251.0 %reduce-scatter.39.cloned.1.call-start = ((), (), s32[]{:S(2)}) async-start(), calls=%async_computation.19 | async-start | bytes 1114112 | tf_op jit(solution)/shard_map/reduce_scatter | solution.py:282
  334.4 246.6 %reduce-scatter.37.cloned.1.call-start = ((), (), s32[]{:S(2)}) async-start(), calls=%async_computation.18 | async-start | bytes 1114112 | tf_op jit(solution)/shard_map/reduce_scatter | solution.py:282
  338.7 312.9 %reduce-scatter.41.cloned.1.call-start = ((), (), s32[]{:S(2)}) async-start(), calls=%async_computation.22 | async-start | bytes 139264
  447.5 8.0 copy-start.13
  447.5 8.0 copy-start.22
  447.5 8.0 copy-start.23
  460.9 16.3 %slice-start = ((s8[16777216]{0:T(1024)(128)(4,1)}), s8[4194304]{0:T(1024)(128)(4,1)S(1)}, s32[]{:S(2)}) async-start(s8[16777216]{0:T(1024)(128)(4,1)} %bitcast.289), calls=%async_computation.32 | async-start | bytes 8388608
  460.9 16.3 %slice-start.1 = ((s8[16777216]{0:T(1024)(128)(4,1)}), s8[4194304]{0:T(1024)(128)(4,1)S(1)}, s32[]{:S(2)}) async-start(s8[16777216]{0:T(1024)(128)(4,1)} %bitcast.289), calls=%async_computation.33 | async-start | bytes 8388608
  460.9 16.3 %slice-start.2 = ((s8[16777216]{0:T(1024)(128)(4,1)}), s8[4194304]{0:T(1024)(128)(4,1)S(1)}, s32[]{:S(2)}) async-start(s8[16777216]{0:T(1024)(128)(4,1)} %bitcast.289), calls=%async_computation.34 | async-start | bytes 8388608
  460.9 16.3 %slice-start.3 = ((s8[16777216]{0:T(1024)(128)(4,1)}), s8[4194304]{0:T(1024)(128)(4,1)S(1)}, s32[]{:S(2)}) async-start(s8[16777216]{0:T(1024)(128)(4,1)} %bitcast.289), calls=%async_computation.35 | async-start | bytes 8388608
  477.2 8.4 copy-start.27
  492.6 9.7 copy-start.39
  502.4 12.3 %copy-start.69 = (bf16[512]{0:T(512)(128)(2,1)S(1)}, bf16[512]{0:T(512)(128)(2,1)}, u32[]{:S(2)}) copy-start(bf16[512]{0:T(512)(128)(2,1)} %get-tuple-element.108) | copy-start | bytes 3076
  502.4 12.4 %copy-start.65 = (bf16[512]{0:T(512)(128)(2,1)S(1)}, bf16[512]{0:T(512)(128)(2,1)}, u32[]{:S(2)}) copy-start(bf16[512]{0:T(512)(128)(2,1)} %get-tuple-element.100) | copy-start | bytes 3076
  515.6 12.6 %copy-start.25 = (bf16[1024,256]{0,1:T(8,128)(2,1)S(1)}, bf16[1024,256]{0,1:T(8,128)(2,1)}, u32[]{:S(2)}) copy-start(bf16[1024,256]{0,1:T(8,128)(2,1)} %copy-done.24) | copy-start | bytes 1572868
  544.2 7.1 copy-start.32
  544.2 8.2 copy-start.3
  544.2 8.2 copy-start.52
  544.2 8.2 copy-start.54
  544.3 8.3 copy-start.59
  544.3 8.3 copy-start.62
  544.3 136.0 %reduce-scatter.43.cloned.1.call-start = ((), (), s32[]{:S(2)}) async-start(), calls=%async_computation.23 | async-start | bytes 139264
  545.2 193.3 %reduce-scatter.31.cloned.1.call-start = ((), (), s32[]{:S(2)}) async-start(), calls=%async_computation.15 | async-start | bytes 278528 | tf_op jit(solution)/shard_map/reduce_scatter | solution.py:276
  552.4 8.2 copy-start.35
  552.4 244.4 %reduce-scatter.29.cloned.1.call-start = ((), (), s32[]{:S(2)}) async-start(), calls=%async_computation.14 | async-start | bytes 278528 | tf_op jit(solution)/shard_map/reduce_scatter | solution.py:276
  556.0 9.8 copy-start.50
  556.0 9.8 copy-start.56
  565.7 331.5 %all-reduce.18.cloned.1.call-start = ((), (), s32[]{:S(2)}) async-start(), calls=%async_computation.29 | async-start | bytes 4194304
  571.7 389.9 %all-reduce.20.cloned.1.call-start = ((), (), s32[]{:S(2)}) async-start(), calls=%async_computation.30 | async-start | bytes 4194304 | tf_op jit(solution)/shard_map/psum | solution.py:195
  575.3 7.3 copy-start.11
  577.3 444.8 %reduce-scatter.45.cloned.1.call-start = ((), (), s32[]{:S(2)}) async-start(), calls=%async_computation.24 | async-start | bytes 139264
  961.7 7.2 copy-start.12
  966.4 113.9 %reduce-scatter.47.cloned.1.call-start = ((), (), s32[]{:S(2)}) async-start(), calls=%async_computation.25 | async-start | bytes 139264
  968.8 169.7 %reduce-scatter.49.cloned.1.call-start = ((), (), s32[]{:S(2)}) async-start(), calls=%async_computation.26 | async-start | bytes 139264
  969.9 226.7 %reduce-scatter.51.cloned.1.call-start = ((), (), s32[]{:S(2)}) async-start(), calls=%async_computation.27 | async-start | bytes 139264
  (42 other events, 169.9 us)
Sparse Core Ops, SparseCore 0:
  157.9 105.1 all-reduce.15
  312.1 62.9 all-reduce.21
  376.6 33.0 all-gather.16
  411.2 33.0 all-gather.14
Sparse Core Ops, SparseCore 1:
  160.4 35.0 all-gather.10
  197.5 36.8 all-gather.12
  325.9 57.3 reduce-scatter.34
  386.9 56.6 reduce-scatter.32
  447.3 56.6 reduce-scatter.38
  507.6 56.6 reduce-scatter.36
  567.6 54.6 reduce-scatter.40
  625.6 54.6 reduce-scatter.42
  683.6 54.8 reduce-scatter.30
  742.0 54.7 reduce-scatter.28
  800.3 96.9 all-reduce.17
  899.6 62.0 all-reduce.19
  966.5 55.6 reduce-scatter.44
  1025.7 54.6 reduce-scatter.46
  1083.8 54.6 reduce-scatter.48
  1142.0 54.6 reduce-scatter.50
